TPU v7x, 32 devices: a whole 2x2x4 slice. The times are simulated.
32 devices in a mesh: mem: 4 (over x, core), tile: 8 (over z, y).
Axes of the slice: x: 2, y: 2, z: 4, core: 2. Of those that a mesh axis runs over, the one named last changes fastest.
Arguments:
- increment: float32 [70, 128, 256], P(None, 'tile')
- previous: float32 [70, 128, 256], P(None, 'tile'), may hold values from -6 to 6
- beta_prev: float32 [1], replicated, may hold values from 0.5 to 1.5
- members: bfloat16 [8, 70, 128, 256], P('mem', None, 'tile'), may hold values from -6 to 6
- band_widths: int32 [70], replicated, may hold values from 1 to 8, as said below
- diffusion_steps: int32 [8], replicated, may hold values from 1 to 4, as said below
Outputs:
- next_vector: float32 [70, 128, 256], P(None, 'tile')
- coefficients: float32 [2], replicated
Inputs may be any that keep to these rules, and one draw needn't show every extreme that they name: `band_widths`: every level's band width lies in the range and some level has exactly 8. `diffusion_steps`: every tile's iteration count lies in the range and some tile has exactly 4.
All inputs are finite; a program needn't handle non-finite values.
Results may differ from a plain program's by a relative error of at most 0.0003.
Values sent between devices are 32-bit elements; how exact they have to be, the bound alone decides.
No kernel may reach another device: no remote copies, remote signals or barrier semaphores. Data moves between devices by JAX's collectives and lax.ppermute only.
A program may use at most 64 MiB of HBM per device.

v0:
```python
import jax
import jax.numpy as jnp
from jax import lax
from jax.sharding import PartitionSpec as P

MEM_DEV = 2
DIFF = 4


def extended(value, sides, width):
    for axis, dim in sides:
        count, length = (lax.axis_size(axis), value.shape[dim])
        up = [(i, (i + 1) % count) for i in range(count - 1)]
        down = [(j, i) for i, j in up]
        last = lax.slice_in_dim(value, length - width, length, axis=dim)
        leading = lax.slice_in_dim(value, 0, width, axis=dim)
        before = lax.ppermute(last, axis, up)
        after = lax.ppermute(leading, axis, down)
        value = jnp.concatenate([before, value, after], axis=dim)
    return value


def vertical_matrix(band_widths):
    levels = jnp.arange(band_widths.shape[0], dtype=jnp.int32)
    apart = levels[:, None] - levels[None, :]
    band_float = band_widths.astype(jnp.float32)
    limit = jnp.minimum(band_widths[:, None], band_widths[None, :])
    weight = jnp.exp(-apart.astype(jnp.float32) ** 2 / (band_float[:, None] * band_float[None, :]))
    return jnp.where(jnp.abs(apart) <= limit, weight, jnp.float32(0.0))


def lanczos_sums(image_part, incr_part, prev_part, beta_value):
    inc_img, inc_inc = lax.psum(
        (jnp.sum(incr_part * image_part), jnp.sum(incr_part * incr_part)), ("mem", "tile")
    )
    alpha_value = inc_img / inc_inc
    residual = image_part - alpha_value * incr_part - beta_value * prev_part
    squares = lax.psum(jnp.sum(residual * residual), ("mem", "tile"))
    return (alpha_value, squares)


def row_owner_counts(diffusion_steps, first_row, row_total, tile_rows):
    global_rows = first_row + jnp.arange(row_total, dtype=jnp.int32)
    owner = jnp.floor_divide(global_rows, tile_rows)
    tile_ids = jnp.arange(diffusion_steps.shape[0], dtype=jnp.int32)
    matches = (owner[:, None] == tile_ids[None, :]).astype(jnp.int32)
    return jnp.sum(matches * diffusion_steps[None, :], axis=1)


def per_device(increment, previous, beta_prev, members, band_widths, diffusion_steps):
    vertical = vertical_matrix(band_widths)
    tile_rows = increment.shape[1]
    tile_here = lax.axis_index("tile")
    members_f = members.astype(jnp.float32)
    localized = jnp.einsum(
        "ij,mjyx->miyx", vertical, members_f * increment[None], precision=lax.Precision.HIGHEST
    )
    step_count = row_owner_counts(diffusion_steps, tile_here * tile_rows, tile_rows, tile_rows)[
        None, None, :, None
    ]
    for sweep_index in range(DIFF):
        padded = extended(localized, (("tile", 2),), 1)
        sideways = jnp.pad(localized, ((0, 0), (0, 0), (0, 0), (1, 1)))
        laplace = (
            padded[:, :, 2:, :]
            + padded[:, :, :-2, :]
            + sideways[:, :, :, 2:]
            + sideways[:, :, :, :-2]
            - 4.0 * localized
        )
        localized = jnp.where(sweep_index < step_count, localized + 0.24 * laplace, localized)
    partial_value = jnp.sum(members_f * localized, axis=0)
    inverse_count = 1.0 / (MEM_DEV * lax.axis_size("mem") - 1)
    beta_value = beta_prev[0]
    cells_all = increment.shape[0] * increment.shape[1] * lax.axis_size("tile") * increment.shape[2]
    share_width = increment.shape[2] // lax.axis_size("mem")
    offset = lax.axis_index("mem") * share_width
    incr_share = lax.dynamic_slice_in_dim(increment, offset, share_width, 2)
    prev_share = lax.dynamic_slice_in_dim(previous, offset, share_width, 2)
    summed = lax.psum(partial_value, "mem")
    image = increment + summed * inverse_count
    image_share = lax.dynamic_slice_in_dim(image, offset, share_width, 2)
    alpha_value, squares = lanczos_sums(image_share, incr_share, prev_share, beta_value)
    scale_value = jnp.sqrt(squares / cells_all + 1e-06)
    residual = image - alpha_value * increment - beta_value * previous
    next_vector = residual / scale_value
    coefficients = jnp.stack([alpha_value, scale_value])
    return (next_vector, coefficients)


def solution(mesh):
    in_specs = (
        P(None, "tile", None),
        P(None, "tile", None),
        P(),
        P("mem", None, "tile", None),
        P(),
        P(),
    )
    out_specs = (P(None, "tile", None), P())
    return jax.shard_map(
        per_device, mesh=mesh, in_specs=in_specs, out_specs=out_specs, check_vma=False
    )
```

profile of v0, /device:TPU:0, one launch (start us, length us, event | category | flops | bytes accessed | tf_op | source)
XLA Modules:
  0.0 210.4 jit_solution(6761432922234523690)
XLA Ops:
  7.2 0.0 all-reduce.7.cloned.1.call-start
  7.2 0.0 copy-start.1
  7.2 2.0 copy.20
  9.2 0.7 convert_element_type.17
  9.9 0.0 copy-done.1
  9.9 0.0 copy-start.4
  9.9 3.4 %fusion.22 = f32[2,70,16,256]{3,1,2,0:T(8,128)S(1)} fusion(f32[70,16,256]{2,0,1:T(8,128)S(1)} %copy.20, bf16[2,70,16,256]{3,2,1,0:T(8,128)(2,1)S(1)} %copy-done.1, f32[70]{0:T(128)S(1)} %convert_element_type.17, s32[70]{0:T(128)} %param.10), kind=kOutput, calls=%fused_computation.44 | convolution fusion | flops 482885472 | bytes 4588080 | tf_op jit(solution)/shard_map/ij,mjyx->miyx/dot_general | solution.py:55
  13.3 0.7 fusion.45
  14.1 1.3 collective-permute-start
  15.4 6.2 %collective-permute-start.1 = (f32[2,70,1,256]{3,1,2,0:T(8,128)}, f32[2,70,1,256]{3,1,2,0:T(8,128)}, u32[]{:S(2)}, u32[]{:S(2)}) collective-permute-start(f32[2,70,1,256]{3,1,2,0:T(8,128)} %get-tuple-element.17), channel_id=1, source_target_pairs={{0,1},{1,2},{2,3},{3,4},{4,5},{5,6},{6,7},{8,9},{9,10},{10,11},{11... | collective-permute-start | bytes 430088 | tf_op jit(solution)/shard_map/ppermute | solution.py:17
  21.5 0.0 copy-done.4
  21.5 0.1 select_reduce_fusion
  21.6 1.5 collective-permute-done
  23.1 3.3 %collective-permute-done.1 = f32[2,70,1,256]{3,1,2,0:T(8,128)} collective-permute-done((f32[2,70,1,256]{3,1,2,0:T(8,128)}, f32[2,70,1,256]{3,1,2,0:T(8,128)}, u32[]{:S(2)}, u32[]{:S(2)}) %collective-permute-start.1) | collective-permute-done | bytes 143392 | tf_op jit(solution)/shard_map/ppermute | solution.py:17
  26.4 2.6 %add_select_fusion.3 = f32[2,70,16,256]{3,1,2,0:T(8,128)S(1)} fusion(f32[2,70,16,256]{3,1,2,0:T(8,128)S(1)} %fusion.22, f32[2,70,1,256]{3,1,2,0:T(8,128)} %collective-permute-done.1, f32[2,70,1,256]{3,1,2,0:T(8,128)} %collective-permute-done, pred[16]{0:T(512)(128)(4,1)S(1)} %get-tuple-element.19), kind=kLoop, calls=%fused_computation.11 | loop fusion | flops 5734400 | bytes 4874256 | tf_op jit(solution)/shard_map/jit(_where)/select_n | solution.py:71
  29.1 1.3 collective-permute-start.2
  30.4 5.0 %collective-permute-start.3 = (f32[2,70,1,256]{3,1,2,0:T(8,128)S(1)}, f32[2,70,1,256]{3,1,2,0:T(8,128)S(1)}, u32[]{:S(2)}, u32[]{:S(2)}) collective-permute-start(f32[2,70,1,256]{3,1,2,0:T(8,128)S(1)} %get-tuple-element.15), channel_id=1, source_target_pairs={{0,1},{1,2},{2,3},{3,4},{4,5},{5,6},{6,7},{8,9},{9,10},{10,11},{11... | collective-permute-start | bytes 430088 | tf_op jit(solution)/shard_map/ppermute | solution.py:17
  35.4 2.1 collective-permute-done.2
  37.5 3.3 %collective-permute-done.3 = f32[2,70,1,256]{3,1,2,0:T(8,128)S(1)} collective-permute-done((f32[2,70,1,256]{3,1,2,0:T(8,128)S(1)}, f32[2,70,1,256]{3,1,2,0:T(8,128)S(1)}, u32[]{:S(2)}, u32[]{:S(2)}) %collective-permute-start.3) | collective-permute-done | bytes 143392 | tf_op jit(solution)/shard_map/ppermute | solution.py:17
  40.8 1.8 add_select_fusion.2
  42.6 1.3 collective-permute-start.4
  43.9 5.0 %collective-permute-start.5 = (f32[2,70,1,256]{3,1,2,0:T(8,128)S(1)}, f32[2,70,1,256]{3,1,2,0:T(8,128)S(1)}, u32[]{:S(2)}, u32[]{:S(2)}) collective-permute-start(f32[2,70,1,256]{3,1,2,0:T(8,128)S(1)} %get-tuple-element.13), channel_id=1, source_target_pairs={{0,1},{1,2},{2,3},{3,4},{4,5},{5,6},{6,7},{8,9},{9,10},{10,11},{11... | collective-permute-start | bytes 430088 | tf_op jit(solution)/shard_map/ppermute | solution.py:17
  48.9 2.1 collective-permute-done.4
  51.0 3.3 %collective-permute-done.5 = f32[2,70,1,256]{3,1,2,0:T(8,128)S(1)} collective-permute-done((f32[2,70,1,256]{3,1,2,0:T(8,128)S(1)}, f32[2,70,1,256]{3,1,2,0:T(8,128)S(1)}, u32[]{:S(2)}, u32[]{:S(2)}) %collective-permute-start.5) | collective-permute-done | bytes 143392 | tf_op jit(solution)/shard_map/ppermute | solution.py:17
  54.3 0.0 copy-start.2
  54.3 1.7 add_select_fusion.1
  56.1 1.3 collective-permute-start.6
  57.4 5.0 %collective-permute-start.7 = (f32[2,70,1,256]{3,1,2,0:T(8,128)S(1)}, f32[2,70,1,256]{3,1,2,0:T(8,128)S(1)}, u32[]{:S(2)}, u32[]{:S(2)}) collective-permute-start(f32[2,70,1,256]{3,1,2,0:T(8,128)S(1)} %get-tuple-element.11), channel_id=1, source_target_pairs={{0,1},{1,2},{2,3},{3,4},{4,5},{5,6},{6,7},{8,9},{9,10},{10,11},{11... | collective-permute-start | bytes 430088 | tf_op jit(solution)/shard_map/ppermute | solution.py:17
  62.4 2.1 collective-permute-done.6
  64.5 3.3 %collective-permute-done.7 = f32[2,70,1,256]{3,1,2,0:T(8,128)S(1)} collective-permute-done((f32[2,70,1,256]{3,1,2,0:T(8,128)S(1)}, f32[2,70,1,256]{3,1,2,0:T(8,128)S(1)}, u32[]{:S(2)}, u32[]{:S(2)}) %collective-permute-start.7) | collective-permute-done | bytes 143392 | tf_op jit(solution)/shard_map/ppermute | solution.py:17
  67.8 0.0 copy-done.2
  67.8 0.0 copy-start.3
  67.8 3.8 %fusion.1 = f32[70,16,256]{2,0,1:T(8,128)} fusion(f32[2,70,16,256]{3,1,2,0:T(8,128)S(1)} %add_select_fusion.1, f32[2,70,1,256]{3,1,2,0:T(8,128)S(1)} %collective-permute-done.7, f32[2,70,1,256]{3,1,2,0:T(8,128)S(1)} %collective-permute-done.6, pred[16]{0:T(512)(128)(4,1)S(1)} %get-tuple-element.18, bf16[2,70,16,256]{3,2,1,0:T(8,128)(2,1)S(1)} %copy-done.2), kind=kLoop, calls=%fused_computation.15 | loop fusion | flops 7168000 | bytes 4874256 | tf_op jit(solution)/shard_map/reduce_sum | solution.py:72
  71.6 0.0 copy-start
  71.6 0.0 all-reduce.7.cloned.1.call-update
  72.4 0.0 copy-done.3
  72.4 1.7 copy.23
  74.1 36.2 %all-reduce.7.cloned.1.call-done = f32[70,16,256]{2,0,1:T(8,128)} async-done(((f32[70,16,256]{2,0,1:T(8,128)}), f32[70,16,256]{2,0,1:T(8,128)}) %all-reduce.7.cloned.1.call-update) | async-done | bytes 1146896 | tf_op jit(solution)/shard_map/psum | solution.py:80
  110.3 0.0 copy-done
  110.4 2.0 multiply_add_fusion
  112.4 1.0 multiply_reduce_fusion.1
  113.3 39.7 %all-reduce.4 = (f32[]{:T(128)}, f32[]{:T(128)}) all-reduce(f32[]{:T(128)} %get-tuple-element.7, f32[]{:T(128)} %get-tuple-element.6), channel_id=1, replica_groups=mesh['mem'=4,'tile'=8] {'mem','tile'}, use_global_device_ids=true, to_apply=%region_4.5 | all-reduce | flops 2 | bytes 16 | tf_op jit(solution)/shard_map/psum | solution.py:33
  154.4 2.2 %multiply_reduce_fusion = f32[]{:T(128)} fusion(f32[70,16,256]{2,0,1:T(8,128)} %copy.23, s32[]{:T(128)S(6)} %select_n.37, f32[70,16,256]{2,0,1:T(8,128)S(1)} %multiply_add_fusion, f32[70,16,256]{2,0,1:T(8,128)S(1)} %copy.20, f32[]{:T(128)} %bitcast.11, f32[]{:T(128)} %div.32), kind=kLoop, calls=%fused_computation.49 | loop fusion | flops 430079 | bytes 860176 | tf_op jit(solution)/shard_map/reduce_sum | solution.py:38
  156.6 41.4 %psum.31 = f32[]{:T(128)} all-reduce(f32[]{:T(128)} %multiply_reduce_fusion), channel_id=1, replica_groups=mesh['mem'=4,'tile'=8] {'mem','tile'}, use_global_device_ids=true, to_apply=%region_8.9 | all-reduce | flops 1 | bytes 8 | tf_op jit(solution)/shard_map/psum | solution.py:38
  198.6 3.0 %subtract_divide_fusion = f32[70,16,256]{2,0,1:T(8,128)S(1)} fusion(f32[]{:T(128)} %sqrt.3, f32[]{:T(128)} %bitcast.10, f32[]{:T(128)} %div.32, f32[70,16,256]{2,1,0:T(8,128)} %param.7, f32[70,16,256]{2,1,0:T(8,128)S(1)} %copy-done, f32[70,16,256]{2,0,1:T(8,128)} %all-reduce.7.cloned.1.call-done), kind=kLoop, calls=%fused_computation.45 | loop fusion | flops 2007040 | bytes 4587532 | tf_op jit(solution)/shard_map/div | solution.py:86
  201.6 1.4 copy.25
  202.9 0.6 pad_maximum_fusion.8
  (5 shorter events, 0.1 us)
Async XLA Ops:
  7.2 103.2 %all-reduce.7.cloned.1.call-start = ((), (), s32[]{:S(2)}) async-start(), calls=%async_computation | async-start | bytes 2359296 | tf_op jit(solution)/shard_map/psum | solution.py:80
  7.2 2.7 %copy-start.1 = (bf16[2,70,16,256]{3,2,1,0:T(8,128)(2,1)S(1)}, bf16[2,70,16,256]{3,2,1,0:T(8,128)(2,1)}, u32[]{:S(2)}) copy-start(bf16[2,70,16,256]{3,2,1,0:T(8,128)(2,1)} %param.9) | copy-start | bytes 3440644
  9.9 11.6 %copy-start.4 = (s32[8]{0:T(128)S(1)}, s32[8]{0:T(128)}, u32[]{:S(2)}) copy-start(s32[8]{0:T(128)} %param.11) | copy-start | bytes 100
  14.1 9.0 %collective-permute-start = (f32[2,70,1,256]{3,1,2,0:T(8,128)}, f32[2,70,1,256]{3,1,2,0:T(8,128)}, u32[]{:S(2)}, u32[]{:S(2)}) collective-permute-start(f32[2,70,1,256]{3,1,2,0:T(8,128)} %get-tuple-element.16), channel_id=1, source_target_pairs={{1,0},{2,1},{3,2},{4,3},{5,4},{6,5},{7,6},{9,8},{10,9},{11,10},{12... | collective-permute-start | bytes 430088 | tf_op jit(solution)/shard_map/ppermute | solution.py:18
  15.4 11.0 %collective-permute-start.1 = (f32[2,70,1,256]{3,1,2,0:T(8,128)}, f32[2,70,1,256]{3,1,2,0:T(8,128)}, u32[]{:S(2)}, u32[]{:S(2)}) collective-permute-start(f32[2,70,1,256]{3,1,2,0:T(8,128)} %get-tuple-element.17), channel_id=1, source_target_pairs={{0,1},{1,2},{2,3},{3,4},{4,5},{5,6},{6,7},{8,9},{9,10},{10,11},{11... | collective-permute-start | bytes 430088 | tf_op jit(solution)/shard_map/ppermute | solution.py:17
  29.1 8.4 %collective-permute-start.2 = (f32[2,70,1,256]{3,1,2,0:T(8,128)S(1)}, f32[2,70,1,256]{3,1,2,0:T(8,128)S(1)}, u32[]{:S(2)}, u32[]{:S(2)}) collective-permute-start(f32[2,70,1,256]{3,1,2,0:T(8,128)S(1)} %get-tuple-element.14), channel_id=1, source_target_pairs={{1,0},{2,1},{3,2},{4,3},{5,4},{6,5},{7,6},{9,8},{10,9},{11,10},{12... | collective-permute-start | bytes 430088 | tf_op jit(solution)/shard_map/ppermute | solution.py:18
  30.4 10.4 %collective-permute-start.3 = (f32[2,70,1,256]{3,1,2,0:T(8,128)S(1)}, f32[2,70,1,256]{3,1,2,0:T(8,128)S(1)}, u32[]{:S(2)}, u32[]{:S(2)}) collective-permute-start(f32[2,70,1,256]{3,1,2,0:T(8,128)S(1)} %get-tuple-element.15), channel_id=1, source_target_pairs={{0,1},{1,2},{2,3},{3,4},{4,5},{5,6},{6,7},{8,9},{9,10},{10,11},{11... | collective-permute-start | bytes 430088 | tf_op jit(solution)/shard_map/ppermute | solution.py:17
  42.6 8.4 %collective-permute-start.4 = (f32[2,70,1,256]{3,1,2,0:T(8,128)S(1)}, f32[2,70,1,256]{3,1,2,0:T(8,128)S(1)}, u32[]{:S(2)}, u32[]{:S(2)}) collective-permute-start(f32[2,70,1,256]{3,1,2,0:T(8,128)S(1)} %get-tuple-element.12), channel_id=1, source_target_pairs={{1,0},{2,1},{3,2},{4,3},{5,4},{6,5},{7,6},{9,8},{10,9},{11,10},{12... | collective-permute-start | bytes 430088 | tf_op jit(solution)/shard_map/ppermute | solution.py:18
  43.9 10.4 %collective-permute-start.5 = (f32[2,70,1,256]{3,1,2,0:T(8,128)S(1)}, f32[2,70,1,256]{3,1,2,0:T(8,128)S(1)}, u32[]{:S(2)}, u32[]{:S(2)}) collective-permute-start(f32[2,70,1,256]{3,1,2,0:T(8,128)S(1)} %get-tuple-element.13), channel_id=1, source_target_pairs={{0,1},{1,2},{2,3},{3,4},{4,5},{5,6},{6,7},{8,9},{9,10},{10,11},{11... | collective-permute-start | bytes 430088 | tf_op jit(solution)/shard_map/ppermute | solution.py:17
  54.3 13.5 %copy-start.2 = (bf16[2,70,16,256]{3,2,1,0:T(8,128)(2,1)S(1)}, bf16[2,70,16,256]{3,2,1,0:T(8,128)(2,1)}, u32[]{:S(2)}) copy-start(bf16[2,70,16,256]{3,2,1,0:T(8,128)(2,1)} %param.9) | copy-start | bytes 3440644
  56.1 8.4 %collective-permute-start.6 = (f32[2,70,1,256]{3,1,2,0:T(8,128)S(1)}, f32[2,70,1,256]{3,1,2,0:T(8,128)S(1)}, u32[]{:S(2)}, u32[]{:S(2)}) collective-permute-start(f32[2,70,1,256]{3,1,2,0:T(8,128)S(1)} %get-tuple-element.10), channel_id=1, source_target_pairs={{1,0},{2,1},{3,2},{4,3},{5,4},{6,5},{7,6},{9,8},{10,9},{11,10},{12... | collective-permute-start | bytes 430088 | tf_op jit(solution)/shard_map/ppermute | solution.py:18
  57.4 10.4 %collective-permute-start.7 = (f32[2,70,1,256]{3,1,2,0:T(8,128)S(1)}, f32[2,70,1,256]{3,1,2,0:T(8,128)S(1)}, u32[]{:S(2)}, u32[]{:S(2)}) collective-permute-start(f32[2,70,1,256]{3,1,2,0:T(8,128)S(1)} %get-tuple-element.11), channel_id=1, source_target_pairs={{0,1},{1,2},{2,3},{3,4},{4,5},{5,6},{6,7},{8,9},{9,10},{10,11},{11... | collective-permute-start | bytes 430088 | tf_op jit(solution)/shard_map/ppermute | solution.py:17
  67.8 4.6 %copy-start.3 = (f32[70,16,256]{2,1,0:T(8,128)S(1)}, f32[70,16,256]{2,1,0:T(8,128)}, u32[]{:S(2)}) copy-start(f32[70,16,256]{2,1,0:T(8,128)} %param.7) | copy-start | bytes 3440644
  71.6 38.7 %copy-start = (f32[70,16,256]{2,1,0:T(8,128)S(1)}, f32[70,16,256]{2,1,0:T(8,128)}, u32[]{:S(2)}) copy-start(f32[70,16,256]{2,1,0:T(8,128)} %param.6) | copy-start | bytes 3440644
Sparse Core Ops, SparseCore 0:
  71.8 38.5 all-reduce.6
where the time goes:
time: 211 us; the launch traced here: 210 us
  blocking collectives  81.1 us (38%)
  waiting for transfers between devices  57.2 us (27%)
  starting transfers between devices  26.4 us (13%)
  other arithmetic  19.4 us (9%)
  between operations  16.9 us (8%)
  local copies, waits for them, and re-layouts  5.91 us (3%)
  matrix products  3.43 us (2%)
    psum x1, blocking collectives, lanczos_sums(): squares = lax.psum(jnp.sum(residual * residual), ('mem', 'tile'))  41.4 us
    psum x1, blocking collectives, lanczos_sums(): lax.psum((jnp.sum(incr_part * image_part), jnp.sum(incr_part * incr_part)...  39.7 us
    psum x1, waiting for transfers between devices, per_device(): summed = lax.psum(partial_value, 'mem')  36.2 us
    ppermute x4, starting transfers between devices, extended(): before = lax.ppermute(last, axis, up)  21.2 us
    ppermute x4, waiting for transfers between devices, extended(): before = lax.ppermute(last, axis, up)  13.2 us
    ppermute x4, waiting for transfers between devices, extended(): after = lax.ppermute(leading, axis, down)  7.71 us
    select_n x3, other arithmetic, per_device(): jnp.where(sweep_index < step_count, localized + 0.24 * laplace, localized)  6.11 us
    ppermute x4, starting transfers between devices, extended(): after = lax.ppermute(leading, axis, down)  5.16 us
  transfers between devices with their start and end apart: 9, of which 9 were waited for; matrix products, arithmetic and copies ran while one was open for 1% of the time, Pallas kernels for 0%

commit v1 on v0

--- a/solution.py
+++ b/solution.py
@@ -31,7 +31,10 @@
 
 def lanczos_sums(image_part, incr_part, prev_part, beta_value):
     inc_img, inc_inc = lax.psum(
-        (jnp.sum(incr_part * image_part), jnp.sum(incr_part * incr_part)), ("mem", "tile")
+        lax.psum(
+            (jnp.sum(incr_part * image_part), jnp.sum(incr_part * incr_part)), axis_name="tile"
+        ),
+        axis_name="mem",
     )
     alpha_value = inc_img / inc_inc
     residual = image_part - alpha_value * incr_part - beta_value * prev_part

time: 211 us -> 196 us (0.929)
  blocking collectives: 81.1 us -> 65.5 us
    psum x1, blocking collectives: 39.7 us -> 22 us  [lanczos_sums(): lax.psum((jnp.sum(incr_part * image_part), jnp.sum(incr_part * incr_part)...]
    psum x0 -> x1, blocking collectives: none -> 6.28 us  [lanczos_sums(): lax.psum(lax.psum((jnp.sum(incr_part * image_part), jnp.sum(incr_part * i...]
    psum x1, blocking collectives: 41.4 us -> 37.2 us  [lanczos_sums(): squares = lax.psum(jnp.sum(residual * residual), ('mem', 'tile'))]
where the time goes in v1:
time: 196 us; the launch traced here: 195 us
  blocking collectives  65.5 us (33%)
  waiting for transfers between devices  57.2 us (29%)
  starting transfers between devices  26.4 us (13%)
  other arithmetic  19.4 us (10%)
  between operations  16.9 us (9%)
  local copies, waits for them, and re-layouts  5.91 us (3%)
  matrix products  3.42 us (2%)
    psum x1, blocking collectives, lanczos_sums(): squares = lax.psum(jnp.sum(residual * residual), ('mem', 'tile'))  37.2 us
    psum x1, waiting for transfers between devices, per_device(): summed = lax.psum(partial_value, 'mem')  36.2 us
    psum x1, blocking collectives, lanczos_sums(): lax.psum((jnp.sum(incr_part * image_part), jnp.sum(incr_part * incr_part)...  22 us
    ppermute x4, starting transfers between devices, extended(): before = lax.ppermute(last, axis, up)  21.2 us
    ppermute x4, waiting for transfers between devices, extended(): before = lax.ppermute(last, axis, up)  13.2 us
    ppermute x4, waiting for transfers between devices, extended(): after = lax.ppermute(leading, axis, down)  7.72 us
    psum x1, blocking collectives, lanczos_sums(): lax.psum(lax.psum((jnp.sum(incr_part * image_part), jnp.sum(incr_part * i...  6.28 us
    select_n x3, other arithmetic, per_device(): jnp.where(sweep_index < step_count, localized + 0.24 * laplace, localized)  6.11 us
  transfers between devices with their start and end apart: 9, of which 9 were waited for; matrix products, arithmetic and copies ran while one was open for 1% of the time, Pallas kernels for 0%

profile of v1, /device:TPU:0, one launch (start us, length us, event | category | flops | bytes accessed | tf_op | source)
XLA Modules:
  0.0 194.8 jit_solution(8323719759936395672)
XLA Ops:
  7.2 0.0 all-reduce.8.cloned.1.call-start
  7.2 0.0 copy-start.1
  7.2 2.0 %copy.20 = f32[70,16,256]{2,0,1:T(8,128)S(1)} copy(f32[70,16,256]{2,1,0:T(8,128)} %param.6) | data formatting | bytes 2293760 | tf_op args[0]
  9.2 0.7 convert_element_type.17
  9.9 0.0 copy-done.1
  9.9 0.0 copy-start.4
  9.9 3.4 %fusion.22 = f32[2,70,16,256]{3,1,2,0:T(8,128)S(1)} fusion(f32[70,16,256]{2,0,1:T(8,128)S(1)} %copy.20, bf16[2,70,16,256]{3,2,1,0:T(8,128)(2,1)S(1)} %copy-done.1, f32[70]{0:T(128)S(1)} %convert_element_type.17, s32[70]{0:T(128)} %param.10), kind=kOutput, calls=%fused_computation.44 | convolution fusion | flops 482885472 | bytes 4588080 | tf_op jit(solution)/shard_map/ij,mjyx->miyx/dot_general | solution.py:58
  13.3 0.7 fusion.45
  14.1 1.3 collective-permute-start
  15.4 6.2 %collective-permute-start.1 = (f32[2,70,1,256]{3,1,2,0:T(8,128)}, f32[2,70,1,256]{3,1,2,0:T(8,128)}, u32[]{:S(2)}, u32[]{:S(2)}) collective-permute-start(f32[2,70,1,256]{3,1,2,0:T(8,128)} %get-tuple-element.19), channel_id=1, source_target_pairs={{0,1},{1,2},{2,3},{3,4},{4,5},{5,6},{6,7},{8,9},{9,10},{10,11},{11... | collective-permute-start | bytes 430088 | tf_op jit(solution)/shard_map/ppermute | solution.py:17
  21.5 0.0 copy-done.4
  21.5 0.1 select_reduce_fusion
  21.6 1.5 collective-permute-done
  23.1 3.3 %collective-permute-done.1 = f32[2,70,1,256]{3,1,2,0:T(8,128)} collective-permute-done((f32[2,70,1,256]{3,1,2,0:T(8,128)}, f32[2,70,1,256]{3,1,2,0:T(8,128)}, u32[]{:S(2)}, u32[]{:S(2)}) %collective-permute-start.1) | collective-permute-done | bytes 143392 | tf_op jit(solution)/shard_map/ppermute | solution.py:17
  26.4 2.6 %add_select_fusion.3 = f32[2,70,16,256]{3,1,2,0:T(8,128)S(1)} fusion(f32[2,70,16,256]{3,1,2,0:T(8,128)S(1)} %fusion.22, f32[2,70,1,256]{3,1,2,0:T(8,128)} %collective-permute-done.1, f32[2,70,1,256]{3,1,2,0:T(8,128)} %collective-permute-done, pred[16]{0:T(512)(128)(4,1)S(1)} %get-tuple-element.21), kind=kLoop, calls=%fused_computation.11 | loop fusion | flops 5734400 | bytes 4874256 | tf_op jit(solution)/shard_map/jit(_where)/select_n | solution.py:74
  29.1 1.3 collective-permute-start.2
  30.4 5.0 %collective-permute-start.3 = (f32[2,70,1,256]{3,1,2,0:T(8,128)S(1)}, f32[2,70,1,256]{3,1,2,0:T(8,128)S(1)}, u32[]{:S(2)}, u32[]{:S(2)}) collective-permute-start(f32[2,70,1,256]{3,1,2,0:T(8,128)S(1)} %get-tuple-element.17), channel_id=1, source_target_pairs={{0,1},{1,2},{2,3},{3,4},{4,5},{5,6},{6,7},{8,9},{9,10},{10,11},{11... | collective-permute-start | bytes 430088 | tf_op jit(solution)/shard_map/ppermute | solution.py:17
  35.4 2.1 %collective-permute-done.2 = f32[2,70,1,256]{3,1,2,0:T(8,128)S(1)} collective-permute-done((f32[2,70,1,256]{3,1,2,0:T(8,128)S(1)}, f32[2,70,1,256]{3,1,2,0:T(8,128)S(1)}, u32[]{:S(2)}, u32[]{:S(2)}) %collective-permute-start.2) | collective-permute-done | bytes 143392 | tf_op jit(solution)/shard_map/ppermute | solution.py:18
  37.5 3.3 %collective-permute-done.3 = f32[2,70,1,256]{3,1,2,0:T(8,128)S(1)} collective-permute-done((f32[2,70,1,256]{3,1,2,0:T(8,128)S(1)}, f32[2,70,1,256]{3,1,2,0:T(8,128)S(1)}, u32[]{:S(2)}, u32[]{:S(2)}) %collective-permute-start.3) | collective-permute-done | bytes 143392 | tf_op jit(solution)/shard_map/ppermute | solution.py:17
  40.8 1.8 add_select_fusion.2
  42.6 1.3 collective-permute-start.4
  43.9 5.0 %collective-permute-start.5 = (f32[2,70,1,256]{3,1,2,0:T(8,128)S(1)}, f32[2,70,1,256]{3,1,2,0:T(8,128)S(1)}, u32[]{:S(2)}, u32[]{:S(2)}) collective-permute-start(f32[2,70,1,256]{3,1,2,0:T(8,128)S(1)} %get-tuple-element.15), channel_id=1, source_target_pairs={{0,1},{1,2},{2,3},{3,4},{4,5},{5,6},{6,7},{8,9},{9,10},{10,11},{11... | collective-permute-start | bytes 430088 | tf_op jit(solution)/shard_map/ppermute | solution.py:17
  48.9 2.1 %collective-permute-done.4 = f32[2,70,1,256]{3,1,2,0:T(8,128)S(1)} collective-permute-done((f32[2,70,1,256]{3,1,2,0:T(8,128)S(1)}, f32[2,70,1,256]{3,1,2,0:T(8,128)S(1)}, u32[]{:S(2)}, u32[]{:S(2)}) %collective-permute-start.4) | collective-permute-done | bytes 143392 | tf_op jit(solution)/shard_map/ppermute | solution.py:18
  51.0 3.3 %collective-permute-done.5 = f32[2,70,1,256]{3,1,2,0:T(8,128)S(1)} collective-permute-done((f32[2,70,1,256]{3,1,2,0:T(8,128)S(1)}, f32[2,70,1,256]{3,1,2,0:T(8,128)S(1)}, u32[]{:S(2)}, u32[]{:S(2)}) %collective-permute-start.5) | collective-permute-done | bytes 143392 | tf_op jit(solution)/shard_map/ppermute | solution.py:17
  54.3 0.0 copy-start.2
  54.3 1.7 add_select_fusion.1
  56.1 1.3 collective-permute-start.6
  57.4 5.0 %collective-permute-start.7 = (f32[2,70,1,256]{3,1,2,0:T(8,128)S(1)}, f32[2,70,1,256]{3,1,2,0:T(8,128)S(1)}, u32[]{:S(2)}, u32[]{:S(2)}) collective-permute-start(f32[2,70,1,256]{3,1,2,0:T(8,128)S(1)} %get-tuple-element.13), channel_id=1, source_target_pairs={{0,1},{1,2},{2,3},{3,4},{4,5},{5,6},{6,7},{8,9},{9,10},{10,11},{11... | collective-permute-start | bytes 430088 | tf_op jit(solution)/shard_map/ppermute | solution.py:17
  62.4 2.1 %collective-permute-done.6 = f32[2,70,1,256]{3,1,2,0:T(8,128)S(1)} collective-permute-done((f32[2,70,1,256]{3,1,2,0:T(8,128)S(1)}, f32[2,70,1,256]{3,1,2,0:T(8,128)S(1)}, u32[]{:S(2)}, u32[]{:S(2)}) %collective-permute-start.6) | collective-permute-done | bytes 143392 | tf_op jit(solution)/shard_map/ppermute | solution.py:18
  64.5 3.3 %collective-permute-done.7 = f32[2,70,1,256]{3,1,2,0:T(8,128)S(1)} collective-permute-done((f32[2,70,1,256]{3,1,2,0:T(8,128)S(1)}, f32[2,70,1,256]{3,1,2,0:T(8,128)S(1)}, u32[]{:S(2)}, u32[]{:S(2)}) %collective-permute-start.7) | collective-permute-done | bytes 143392 | tf_op jit(solution)/shard_map/ppermute | solution.py:17
  67.8 0.0 copy-done.2
  67.8 0.0 copy-start.3
  67.8 3.8 %fusion.1 = f32[70,16,256]{2,0,1:T(8,128)} fusion(f32[2,70,16,256]{3,1,2,0:T(8,128)S(1)} %add_select_fusion.1, f32[2,70,1,256]{3,1,2,0:T(8,128)S(1)} %collective-permute-done.7, f32[2,70,1,256]{3,1,2,0:T(8,128)S(1)} %collective-permute-done.6, pred[16]{0:T(512)(128)(4,1)S(1)} %get-tuple-element.20, bf16[2,70,16,256]{3,2,1,0:T(8,128)(2,1)S(1)} %copy-done.2), kind=kLoop, calls=%fused_computation.15 | loop fusion | flops 7168000 | bytes 4874256 | tf_op jit(solution)/shard_map/reduce_sum | solution.py:75
  71.6 0.0 copy-start
  71.6 0.0 all-reduce.8.cloned.1.call-update
  72.4 0.0 copy-done.3
  72.4 1.7 copy.23
  74.1 36.2 %all-reduce.8.cloned.1.call-done = f32[70,16,256]{2,0,1:T(8,128)} async-done(((f32[70,16,256]{2,0,1:T(8,128)}), f32[70,16,256]{2,0,1:T(8,128)}) %all-reduce.8.cloned.1.call-update) | async-done | bytes 1146896 | tf_op jit(solution)/shard_map/psum | solution.py:83
  110.3 0.0 copy-done
  110.3 2.0 %multiply_add_fusion = f32[70,16,256]{2,0,1:T(8,128)S(1)} fusion(f32[70,16,256]{2,0,1:T(8,128)} %all-reduce.8.cloned.1.call-done, f32[70,16,256]{2,1,0:T(8,128)S(1)} %copy-done), kind=kLoop, calls=%fused_computation.46 | loop fusion | flops 573440 | bytes 3440640 | tf_op jit(solution)/shard_map/add | solution.py:84
  112.3 1.0 multiply_reduce_fusion.1
  113.3 22.0 %all-reduce.4 = (f32[]{:T(128)}, f32[]{:T(128)}) all-reduce(f32[]{:T(128)} %get-tuple-element.7, f32[]{:T(128)} %get-tuple-element.6), channel_id=1, replica_groups=mesh['mem'=4,'tile'=8] {'tile'}, use_global_device_ids=true, to_apply=%region_4.5 | all-reduce | flops 2 | bytes 16 | tf_op jit(solution)/shard_map/psum | solution.py:34
  135.4 6.3 %all-reduce.5 = (f32[]{:T(128)}, f32[]{:T(128)}) all-reduce(f32[]{:T(128)} %get-tuple-element.8, f32[]{:T(128)} %get-tuple-element.9), channel_id=1, replica_groups=mesh['mem'=4,'tile'=8] {'mem'}, use_global_device_ids=true, to_apply=%region_5.6 | all-reduce | flops 2 | bytes 16 | tf_op jit(solution)/shard_map/psum | solution.py:33
  143.0 2.2 %multiply_reduce_fusion = f32[]{:T(128)} fusion(f32[70,16,256]{2,0,1:T(8,128)} %copy.23, s32[]{:T(128)S(6)} %select_n.37, f32[70,16,256]{2,0,1:T(8,128)S(1)} %multiply_add_fusion, f32[70,16,256]{2,0,1:T(8,128)S(1)} %copy.20, f32[]{:T(128)} %bitcast.11, f32[]{:T(128)} %div.32), kind=kLoop, calls=%fused_computation.49 | loop fusion | flops 430079 | bytes 860176 | tf_op jit(solution)/shard_map/reduce_sum | solution.py:41
  145.2 37.2 %psum.47 = f32[]{:T(128)} all-reduce(f32[]{:T(128)} %multiply_reduce_fusion), channel_id=1, replica_groups=mesh['mem'=4,'tile'=8] {'mem','tile'}, use_global_device_ids=true, to_apply=%region_10.11 | all-reduce | flops 1 | bytes 8 | tf_op jit(solution)/shard_map/psum | solution.py:41
  183.1 3.0 %subtract_divide_fusion = f32[70,16,256]{2,0,1:T(8,128)S(1)} fusion(f32[]{:T(128)} %sqrt.3, f32[]{:T(128)} %bitcast.10, f32[]{:T(128)} %div.32, f32[70,16,256]{2,1,0:T(8,128)} %param.7, f32[70,16,256]{2,1,0:T(8,128)S(1)} %copy-done, f32[70,16,256]{2,0,1:T(8,128)} %all-reduce.8.cloned.1.call-done), kind=kLoop, calls=%fused_computation.45 | loop fusion | flops 2007040 | bytes 4587532 | tf_op jit(solution)/shard_map/div | solution.py:89
  186.1 1.4 copy.25
  187.4 0.6 pad_maximum_fusion.8
  (5 shorter events, 0.1 us)
Async XLA Ops:
  7.2 103.2 %all-reduce.8.cloned.1.call-start = ((), (), s32[]{:S(2)}) async-start(), calls=%async_computation | async-start | bytes 2359296 | tf_op jit(solution)/shard_map/psum | solution.py:83
  7.2 2.7 %copy-start.1 = (bf16[2,70,16,256]{3,2,1,0:T(8,128)(2,1)S(1)}, bf16[2,70,16,256]{3,2,1,0:T(8,128)(2,1)}, u32[]{:S(2)}) copy-start(bf16[2,70,16,256]{3,2,1,0:T(8,128)(2,1)} %param.9) | copy-start | bytes 3440644
  9.9 11.6 %copy-start.4 = (s32[8]{0:T(128)S(1)}, s32[8]{0:T(128)}, u32[]{:S(2)}) copy-start(s32[8]{0:T(128)} %param.11) | copy-start | bytes 100
  14.1 9.0 %collective-permute-start = (f32[2,70,1,256]{3,1,2,0:T(8,128)}, f32[2,70,1,256]{3,1,2,0:T(8,128)}, u32[]{:S(2)}, u32[]{:S(2)}) collective-permute-start(f32[2,70,1,256]{3,1,2,0:T(8,128)} %get-tuple-element.18), channel_id=1, source_target_pairs={{1,0},{2,1},{3,2},{4,3},{5,4},{6,5},{7,6},{9,8},{10,9},{11,10},{12... | collective-permute-start | bytes 430088 | tf_op jit(solution)/shard_map/ppermute | solution.py:18
  15.4 11.0 %collective-permute-start.1 = (f32[2,70,1,256]{3,1,2,0:T(8,128)}, f32[2,70,1,256]{3,1,2,0:T(8,128)}, u32[]{:S(2)}, u32[]{:S(2)}) collective-permute-start(f32[2,70,1,256]{3,1,2,0:T(8,128)} %get-tuple-element.19), channel_id=1, source_target_pairs={{0,1},{1,2},{2,3},{3,4},{4,5},{5,6},{6,7},{8,9},{9,10},{10,11},{11... | collective-permute-start | bytes 430088 | tf_op jit(solution)/shard_map/ppermute | solution.py:17
  29.1 8.4 %collective-permute-start.2 = (f32[2,70,1,256]{3,1,2,0:T(8,128)S(1)}, f32[2,70,1,256]{3,1,2,0:T(8,128)S(1)}, u32[]{:S(2)}, u32[]{:S(2)}) collective-permute-start(f32[2,70,1,256]{3,1,2,0:T(8,128)S(1)} %get-tuple-element.16), channel_id=1, source_target_pairs={{1,0},{2,1},{3,2},{4,3},{5,4},{6,5},{7,6},{9,8},{10,9},{11,10},{12... | collective-permute-start | bytes 430088 | tf_op jit(solution)/shard_map/ppermute | solution.py:18
  30.4 10.4 %collective-permute-start.3 = (f32[2,70,1,256]{3,1,2,0:T(8,128)S(1)}, f32[2,70,1,256]{3,1,2,0:T(8,128)S(1)}, u32[]{:S(2)}, u32[]{:S(2)}) collective-permute-start(f32[2,70,1,256]{3,1,2,0:T(8,128)S(1)} %get-tuple-element.17), channel_id=1, source_target_pairs={{0,1},{1,2},{2,3},{3,4},{4,5},{5,6},{6,7},{8,9},{9,10},{10,11},{11... | collective-permute-start | bytes 430088 | tf_op jit(solution)/shard_map/ppermute | solution.py:17
  42.6 8.4 %collective-permute-start.4 = (f32[2,70,1,256]{3,1,2,0:T(8,128)S(1)}, f32[2,70,1,256]{3,1,2,0:T(8,128)S(1)}, u32[]{:S(2)}, u32[]{:S(2)}) collective-permute-start(f32[2,70,1,256]{3,1,2,0:T(8,128)S(1)} %get-tuple-element.14), channel_id=1, source_target_pairs={{1,0},{2,1},{3,2},{4,3},{5,4},{6,5},{7,6},{9,8},{10,9},{11,10},{12... | collective-permute-start | bytes 430088 | tf_op jit(solution)/shard_map/ppermute | solution.py:18
  43.9 10.4 %collective-permute-start.5 = (f32[2,70,1,256]{3,1,2,0:T(8,128)S(1)}, f32[2,70,1,256]{3,1,2,0:T(8,128)S(1)}, u32[]{:S(2)}, u32[]{:S(2)}) collective-permute-start(f32[2,70,1,256]{3,1,2,0:T(8,128)S(1)} %get-tuple-element.15), channel_id=1, source_target_pairs={{0,1},{1,2},{2,3},{3,4},{4,5},{5,6},{6,7},{8,9},{9,10},{10,11},{11... | collective-permute-start | bytes 430088 | tf_op jit(solution)/shard_map/ppermute | solution.py:17
  54.3 13.5 %copy-start.2 = (bf16[2,70,16,256]{3,2,1,0:T(8,128)(2,1)S(1)}, bf16[2,70,16,256]{3,2,1,0:T(8,128)(2,1)}, u32[]{:S(2)}) copy-start(bf16[2,70,16,256]{3,2,1,0:T(8,128)(2,1)} %param.9) | copy-start | bytes 3440644
  56.1 8.4 %collective-permute-start.6 = (f32[2,70,1,256]{3,1,2,0:T(8,128)S(1)}, f32[2,70,1,256]{3,1,2,0:T(8,128)S(1)}, u32[]{:S(2)}, u32[]{:S(2)}) collective-permute-start(f32[2,70,1,256]{3,1,2,0:T(8,128)S(1)} %get-tuple-element.12), channel_id=1, source_target_pairs={{1,0},{2,1},{3,2},{4,3},{5,4},{6,5},{7,6},{9,8},{10,9},{11,10},{12... | collective-permute-start | bytes 430088 | tf_op jit(solution)/shard_map/ppermute | solution.py:18
  57.4 10.4 %collective-permute-start.7 = (f32[2,70,1,256]{3,1,2,0:T(8,128)S(1)}, f32[2,70,1,256]{3,1,2,0:T(8,128)S(1)}, u32[]{:S(2)}, u32[]{:S(2)}) collective-permute-start(f32[2,70,1,256]{3,1,2,0:T(8,128)S(1)} %get-tuple-element.13), channel_id=1, source_target_pairs={{0,1},{1,2},{2,3},{3,4},{4,5},{5,6},{6,7},{8,9},{9,10},{10,11},{11... | collective-permute-start | bytes 430088 | tf_op jit(solution)/shard_map/ppermute | solution.py:17
  67.8 4.6 %copy-start.3 = (f32[70,16,256]{2,1,0:T(8,128)S(1)}, f32[70,16,256]{2,1,0:T(8,128)}, u32[]{:S(2)}) copy-start(f32[70,16,256]{2,1,0:T(8,128)} %param.7) | copy-start | bytes 3440644
  71.6 38.7 %copy-start = (f32[70,16,256]{2,1,0:T(8,128)S(1)}, f32[70,16,256]{2,1,0:T(8,128)}, u32[]{:S(2)}) copy-start(f32[70,16,256]{2,1,0:T(8,128)} %param.6) | copy-start | bytes 3440644
Sparse Core Ops, SparseCore 0:
  71.8 38.5 all-reduce.7
